TPU v7x, 32 devices: a whole 2x2x4 slice. The times are simulated.
32 devices in a mesh: groups: 2 (over y), vox: 4 (over z), chan: 2 (over x), frm: 2 (over core).
Axes of the slice: x: 2, y: 2, z: 4, core: 2. Of those that a mesh axis runs over, the one named last changes fastest.
Arguments:
- echo_data: bfloat16 [8, 2, 1024, 2, 512], P(('groups', 'vox'), 'chan', None, None, 'frm'), parts along dimension 0, may hold values from -36 to 36
- tile_weights: bfloat16 [4, 2, 64, 128, 128], P('vox', 'chan'), may hold values from -0.0625 to 0.0625
- tile_target: int32 [4, 2, 64], P('vox', 'chan'), may hold values from 0 to 1
- tile_offset: int32 [4, 2, 64], P('vox', 'chan'), may hold values from 0 to 896
- tile_count: int32 [4, 2], P('vox', 'chan'), may hold values from 8 to 64, as said below
- grid_map: int32 [4, 256], P('vox'), may hold values from 0 to 255, each once within a row
- psf_kernel: float32 [5, 5], replicated, may hold values from -1.25 to 1.25
Outputs:
- psf_image: float32 [64, 32, 512], P(('groups', 'vox'), 'chan', 'frm'), parts along dimension 0
There are 2 independent parts, one for each index of `groups`. A program takes and returns all parts, laid end to end along the dimension named above; an argument that names none is the same for every part. Nothing has to cross between parts.
Inputs may be any that keep to these rules, and one draw needn't show every extreme that they name: `tile_count`: in each voxel block exactly one channel group uses all 64 slots; the others use far fewer. `grid_map`: each block's row is a permutation of 0 to 255.
All inputs are finite; a program needn't handle non-finite values.
Results may differ from a plain program's by a relative error of at most 0.014.
Values may be sent and summed in bfloat16 or wider, within the bound.
A program may use at most 64 MiB of HBM per device.

v0:
```python
import jax
import jax.numpy as jnp
from jax import lax
from jax.sharding import PartitionSpec as P

TBATCH = 8
LAT_DEV = 8


POLY_COEFFS = (1.0, -0.6, 0.15, -0.03)


def with_halo(shard, sides, width):
    for axis, dim in sides:
        devices, length = (lax.axis_size(axis), shard.shape[dim])
        up = [(i, (i + 1) % devices) for i in range(devices - 1)]
        down = [(j, i) for i, j in up]
        last = lax.slice_in_dim(shard, length - width, length, axis=dim)
        leading = lax.slice_in_dim(shard, 0, width, axis=dim)
        before = lax.ppermute(last, axis, up)
        after = lax.ppermute(leading, axis, down)
        shard = jnp.concatenate([before, shard, after], axis=dim)
    return shard


def complex_times(left_real, left_imag, right_real, right_imag):
    level = lax.Precision.HIGH
    real_part = jnp.dot(
        left_real, right_real, precision=level, preferred_element_type=jnp.float32
    ) - jnp.dot(left_imag, right_imag, precision=level, preferred_element_type=jnp.float32)
    imag_part = jnp.dot(
        left_real, right_imag, precision=level, preferred_element_type=jnp.float32
    ) + jnp.dot(left_imag, right_real, precision=level, preferred_element_type=jnp.float32)
    return (real_part, imag_part)


def tile_pass(flat_echo, weights, tile_goal, tile_start, live_total, tiles_out):
    tile_size = weights.shape[-1]
    col_count = flat_echo.shape[-1]
    slot_count = weights.shape[0]
    lane_ids = jnp.arange(TBATCH, dtype=jnp.int32)
    target_ids = jnp.arange(tiles_out, dtype=jnp.int32)
    zero_index = jnp.zeros((), jnp.int32)

    def cut_rows(offset_id):
        return lax.dynamic_slice(flat_echo, (offset_id, zero_index), (tile_size, col_count))

    def one_turn(turn_index, totals):
        where_at = turn_index * TBATCH + lane_ids
        live_lane = where_at < live_total
        chosen = jnp.minimum(where_at, slot_count - 1)
        picked = weights[chosen]
        samples = jax.vmap(cut_rows)(tile_start[chosen])
        product = jnp.einsum("krs,ksc->krc", picked, samples, preferred_element_type=jnp.float32)
        placing = ((tile_goal[chosen][:, None] == target_ids[None, :]) & live_lane[:, None]).astype(
            jnp.float32
        )
        return totals + jnp.einsum("kt,krc->trc", placing, product)

    start_totals = jnp.zeros((tiles_out, tile_size, col_count), jnp.float32)
    turn_count = (live_total + TBATCH - 1) // TBATCH
    return lax.fori_loop(0, turn_count, one_turn, start_totals)


def shards(echo_data, tile_weights, tile_target, tile_offset, tile_count, grid_map, psf_kernel):
    row_count = echo_data.shape[2]
    half_frames = echo_data.shape[4]
    tile_size = tile_weights.shape[-1]
    slot_count = tile_weights.shape[2]
    voxels = grid_map.shape[1]
    tiles_out = voxels // tile_size
    flat_echo = echo_data.reshape(row_count, 2 * half_frames)
    weights = tile_weights.reshape(slot_count, tile_size, tile_size)
    tile_sums = tile_pass(
        flat_echo,
        weights,
        tile_target.reshape(-1),
        tile_offset.reshape(-1),
        tile_count[0, 0],
        tiles_out,
    )
    arranged = jnp.take(tile_sums.reshape(voxels, 2, half_frames), grid_map[0], axis=0)
    arranged = arranged.reshape(LAT_DEV, voxels // LAT_DEV, 2, half_frames)
    beamformed = lax.psum_scatter(arranged, "chan", scatter_dimension=1, tiled=True).astype(
        jnp.bfloat16
    )
    lat_count = beamformed.shape[0]
    depth_count = beamformed.shape[1]
    cell_count = lat_count * depth_count
    own_frames = beamformed.reshape(cell_count, 2, half_frames)
    all_frames = lax.all_gather(own_frames, "frm", axis=2, tiled=True)
    frames = all_frames.shape[2]
    own_flat = own_frames.reshape(cell_count, 2 * half_frames)
    all_flat = all_frames.reshape(cell_count, 2 * frames)
    gram_block = lax.dot_general(
        own_flat, all_flat, (((0,), (0,)), ((), ())), preferred_element_type=jnp.float32
    )
    gram_real = gram_block[:half_frames, :frames] + gram_block[half_frames:, frames:]
    gram_imag = gram_block[:half_frames, frames:] - gram_block[half_frames:, :frames]
    frame_start = lax.axis_index("frm") * half_frames
    echo_real = all_frames[:, 0, :].astype(jnp.float32)
    echo_imag = all_frames[:, 1, :].astype(jnp.float32)
    energy = jnp.sum(echo_real * echo_real + echo_imag * echo_imag)
    gram_real, gram_imag, trace_value = lax.psum((gram_real, gram_imag, energy), ("vox", "chan"))
    factor = frames / trace_value
    norm_real = factor * gram_real
    norm_imag = factor * gram_imag
    full_real, full_imag = (
        lax.all_gather(norm_real, "frm", axis=0, tiled=True),
        lax.all_gather(norm_imag, "frm", axis=0, tiled=True),
    )
    identity = jnp.eye(frames, dtype=jnp.float32)
    poly_real = POLY_COEFFS[3] * full_real + POLY_COEFFS[2] * identity
    poly_imag = POLY_COEFFS[3] * full_imag
    poly_real, poly_imag = complex_times(poly_real, poly_imag, full_real, full_imag)
    poly_real = poly_real + POLY_COEFFS[1] * identity
    cols_real = lax.dynamic_slice_in_dim(full_real, frame_start, half_frames, 1)
    cols_imag = lax.dynamic_slice_in_dim(full_imag, frame_start, half_frames, 1)
    filter_real, filter_imag = complex_times(poly_real, poly_imag, cols_real, cols_imag)
    filter_real = filter_real + POLY_COEFFS[0] * lax.dynamic_slice_in_dim(
        identity, frame_start, half_frames, 1
    )
    out_real, out_imag = complex_times(echo_real, echo_imag, filter_real, filter_imag)
    envelope = jnp.sqrt(out_real * out_real + out_imag * out_imag + 1e-06)
    envelope = envelope.reshape(lat_count, depth_count, half_frames)
    padded = with_halo(envelope, (("vox", 0), ("chan", 1)), 2)
    psf_image = jnp.zeros_like(envelope)
    for shift_a in range(5):
        for shift_b in range(5):
            psf_image = (
                psf_image
                + psf_kernel[shift_a, shift_b]
                * padded[shift_a : shift_a + lat_count, shift_b : shift_b + depth_count]
            )
    return psf_image


def solution(mesh):
    in_specs = (
        P(("groups", "vox"), "chan", None, None, "frm"),
        P("vox", "chan", None, None, None),
        P("vox", "chan", None),
        P("vox", "chan", None),
        P("vox", "chan"),
        P("vox", None),
        P(),
    )
    out_specs = P(("groups", "vox"), "chan", "frm")
    return jax.shard_map(shards, mesh=mesh, in_specs=in_specs, out_specs=out_specs, check_vma=False)
```

profile of v0, /device:TPU:0, one launch (start us, length us, event | category | flops | bytes accessed | tf_op | source)
XLA Modules:
  0.0 305.5 jit_solution(13649038592146255879)
XLA Ops:
  8.5 1.3 reduce.3
  10.0 1.5 copy.32
  11.6 120.6 %while.15 = (s32[]{:T(128)}, f32[2,128,512]{2,0,1:T(2,128)S(1)}, s32[]{:T(128)}, s32[64]{0:T(128)S(1)}, s32[]{:T(128)}, /*index=5*/bf16[64,128,128]{2,1,0:T(8,12...) while((s32[]{:T(128)}, f32[2,128,512]{2,0,1:T(2,128)S(1)}, ...), condition=%wide.region_1.2_spmd.clone, body=%wide.region_0.1_spmd.clone.sunk | while | flops 136447088 | bytes 5247770 | solution.py:62
  13.6 2.2 gather_fusion
  15.8 9.3 %while.16 = (s32[]{:T(128)}, bf16[1024,512]{1,0:T(8,128)(2,1)S(1)}, s32[8,2]{0,1:T(2,128)S(1)}, bf16[8,128,512]{2,1,0:T(8,128)(2,1)S(1)}, s32[]{:T(128)}) while((s32[]{:T(128)}, bf16[1024,512]{1,0:T(8,128)(2,1)S(1)}, s32[8,2]{0,1:T(2,128)S(1)}, bf16[8,128,512]{2,1,0:T(8,128)(2,1)S(1)}, s32[]{:T(128)}) %tuple.64), condition=%wide.while_cond, body=%wide.while_body.sunk | while | flops 2 | bytes 262249 | solution.py:46
  25.6 1.1 fusion.133
  28.7 2.2 gather_fusion
  30.9 9.3 %while.16 = (s32[]{:T(128)}, bf16[1024,512]{1,0:T(8,128)(2,1)S(1)}, s32[8,2]{0,1:T(2,128)S(1)}, bf16[8,128,512]{2,1,0:T(8,128)(2,1)S(1)}, s32[]{:T(128)}) while((s32[]{:T(128)}, bf16[1024,512]{1,0:T(8,128)(2,1)S(1)}, s32[8,2]{0,1:T(2,128)S(1)}, bf16[8,128,512]{2,1,0:T(8,128)(2,1)S(1)}, s32[]{:T(128)}) %tuple.64), condition=%wide.while_cond, body=%wide.while_body.sunk | while | flops 2 | bytes 262249 | solution.py:46
  40.6 1.1 fusion.133
  43.8 2.2 gather_fusion
  46.0 9.3 %while.16 = (s32[]{:T(128)}, bf16[1024,512]{1,0:T(8,128)(2,1)S(1)}, s32[8,2]{0,1:T(2,128)S(1)}, bf16[8,128,512]{2,1,0:T(8,128)(2,1)S(1)}, s32[]{:T(128)}) while((s32[]{:T(128)}, bf16[1024,512]{1,0:T(8,128)(2,1)S(1)}, s32[8,2]{0,1:T(2,128)S(1)}, bf16[8,128,512]{2,1,0:T(8,128)(2,1)S(1)}, s32[]{:T(128)}) %tuple.64), condition=%wide.while_cond, body=%wide.while_body.sunk | while | flops 2 | bytes 262249 | solution.py:46
  55.7 1.1 fusion.133
  58.8 2.2 gather_fusion
  61.0 9.3 %while.16 = (s32[]{:T(128)}, bf16[1024,512]{1,0:T(8,128)(2,1)S(1)}, s32[8,2]{0,1:T(2,128)S(1)}, bf16[8,128,512]{2,1,0:T(8,128)(2,1)S(1)}, s32[]{:T(128)}) while((s32[]{:T(128)}, bf16[1024,512]{1,0:T(8,128)(2,1)S(1)}, s32[8,2]{0,1:T(2,128)S(1)}, bf16[8,128,512]{2,1,0:T(8,128)(2,1)S(1)}, s32[]{:T(128)}) %tuple.64), condition=%wide.while_cond, body=%wide.while_body.sunk | while | flops 2 | bytes 262249 | solution.py:46
  70.8 1.1 fusion.133
  73.9 2.2 gather_fusion
  76.1 9.3 %while.16 = (s32[]{:T(128)}, bf16[1024,512]{1,0:T(8,128)(2,1)S(1)}, s32[8,2]{0,1:T(2,128)S(1)}, bf16[8,128,512]{2,1,0:T(8,128)(2,1)S(1)}, s32[]{:T(128)}) while((s32[]{:T(128)}, bf16[1024,512]{1,0:T(8,128)(2,1)S(1)}, s32[8,2]{0,1:T(2,128)S(1)}, bf16[8,128,512]{2,1,0:T(8,128)(2,1)S(1)}, s32[]{:T(128)}) %tuple.64), condition=%wide.while_cond, body=%wide.while_body.sunk | while | flops 2 | bytes 262249 | solution.py:46
  85.9 1.1 fusion.133
  89.0 2.2 gather_fusion
  91.2 9.3 %while.16 = (s32[]{:T(128)}, bf16[1024,512]{1,0:T(8,128)(2,1)S(1)}, s32[8,2]{0,1:T(2,128)S(1)}, bf16[8,128,512]{2,1,0:T(8,128)(2,1)S(1)}, s32[]{:T(128)}) while((s32[]{:T(128)}, bf16[1024,512]{1,0:T(8,128)(2,1)S(1)}, s32[8,2]{0,1:T(2,128)S(1)}, bf16[8,128,512]{2,1,0:T(8,128)(2,1)S(1)}, s32[]{:T(128)}) %tuple.64), condition=%wide.while_cond, body=%wide.while_body.sunk | while | flops 2 | bytes 262249 | solution.py:46
  100.9 1.1 fusion.133
  104.1 2.2 gather_fusion
  106.3 9.3 %while.16 = (s32[]{:T(128)}, bf16[1024,512]{1,0:T(8,128)(2,1)S(1)}, s32[8,2]{0,1:T(2,128)S(1)}, bf16[8,128,512]{2,1,0:T(8,128)(2,1)S(1)}, s32[]{:T(128)}) while((s32[]{:T(128)}, bf16[1024,512]{1,0:T(8,128)(2,1)S(1)}, s32[8,2]{0,1:T(2,128)S(1)}, bf16[8,128,512]{2,1,0:T(8,128)(2,1)S(1)}, s32[]{:T(128)}) %tuple.64), condition=%wide.while_cond, body=%wide.while_body.sunk | while | flops 2 | bytes 262249 | solution.py:46
  116.0 1.1 fusion.133
  119.1 2.2 gather_fusion
  121.3 9.3 %while.16 = (s32[]{:T(128)}, bf16[1024,512]{1,0:T(8,128)(2,1)S(1)}, s32[8,2]{0,1:T(2,128)S(1)}, bf16[8,128,512]{2,1,0:T(8,128)(2,1)S(1)}, s32[]{:T(128)}) while((s32[]{:T(128)}, bf16[1024,512]{1,0:T(8,128)(2,1)S(1)}, s32[8,2]{0,1:T(2,128)S(1)}, bf16[8,128,512]{2,1,0:T(8,128)(2,1)S(1)}, s32[]{:T(128)}) %tuple.64), condition=%wide.while_cond, body=%wide.while_body.sunk | while | flops 2 | bytes 262249 | solution.py:46
  131.1 1.1 fusion.133
  132.7 1.2 gather_fusion.3
  133.9 1.1 copy_select_fusion
  135.1 16.5 %reduce-scatter.2.cloned.1.call-done = f32[8,16,2,256]{3,0,2,1:T(8,128)} async-done(((f32[8,32,2,256]{3,0,2,1:T(8,128)}), f32[8,16,2,256]{3,0,2,1:T(8,128)}) %reduce-scatter.2.cloned.1.call-update) | async-done | bytes 262160 | tf_op jit(solution)/shard_map/reduce_scatter | solution.py:84
  152.8 2.0 all_gather.9
  155.5 1.2 slice_subtract_fusion
  157.4 21.4 %psum.21 = f32[]{:T(128)} all-reduce(f32[]{:T(128)} %add_reduce_fusion), channel_id=1, replica_groups=mesh['groups'=2,'vox'=4,'chan'=2,'frm'=2] {'vox','chan'}, use_global_device_ids=true, to_apply=%region_4.5 | all-reduce | flops 1 | bytes 8 | tf_op jit(solution)/shard_map/psum | solution.py:104
  179.4 55.8 %all-reduce.4.cloned.1.call-done = (f32[256,512]{1,0:T(8,128)}, f32[256,512]{1,0:T(8,128)}) async-done(((f32[256,512]{1,0:T(8,128)}, f32[256,512]{1,0:T(8,128)}), (f32[256,512]{1,0:T(8,128)}, f32[256,512]{1,0:T(8,128)})) %all-reduce.4.cloned.1.call-update) | async-done | bytes 1048592 | tf_op jit(solution)/shard_map/psum | solution.py:104
  235.2 1.9 broadcast_multiply_fusion.1
  237.4 1.9 broadcast_multiply_fusion
  239.4 6.6 %all-gather.3.cloned.1.call-done = f32[512,512]{1,0:T(8,128)} async-done(((f32[256,512]{1,0:T(8,128)}), f32[512,512]{1,0:T(8,128)}) %all-gather.3.cloned.1.call-update) | async-done | bytes 1048592 | tf_op jit(solution)/shard_map/all_gather | solution.py:109
  246.0 2.7 fusion.38
  248.7 8.9 %all-gather.5.cloned.1.call-done = f32[512,512]{1,0:T(8,128)} async-done(((f32[256,512]{1,0:T(8,128)}), f32[512,512]{1,0:T(8,128)}) %all-gather.5.cloned.1.call-update) | async-done | bytes 1048592 | tf_op jit(solution)/shard_map/all_gather | solution.py:110
  257.6 2.3 fusion.37
  259.9 1.0 fusion.28
  261.0 1.0 fusion.25
  265.5 1.3 collective-permute-start.1
  266.8 4.5 %collective-permute-start = (f32[2,16,256]{2,1,0:T(8,128)S(1)}, f32[2,16,256]{2,1,0:T(8,128)S(1)}, u32[]{:S(2)}, u32[]{:S(2)}) collective-permute-start(f32[2,16,256]{2,1,0:T(8,128)S(1)} %bitcast.114), channel_id=1, source_target_pairs={{0,4},{4,8},{8,12},{1,5},{5,9},{9,13},{2,6},{6,10},{10,14},{3,7},{... | collective-permute-start | bytes 98312 | tf_op jit(solution)/shard_map/ppermute | solution.py:20
  272.9 3.6 %collective-permute-start.2 = (f32[12,2,256]{2,1,0:T(2,128)S(1)}, f32[12,2,256]{2,1,0:T(2,128)S(1)}, u32[]{:S(2)}, u32[]{:S(2)}) collective-permute-start(f32[12,2,256]{2,1,0:T(2,128)S(1)} %get-tuple-element.118), channel_id=1, source_target_pairs={{0,2},{1,3},{4,6},{5,7},{8,10},{9,11},{12,14},{13,15},{16,18},{17,... | collective-permute-start | bytes 73736 | tf_op jit(solution)/shard_map/ppermute | solution.py:20
  276.6 1.3 collective-permute-start.3
  278.6 3.7 %collective-permute-done.3 = f32[12,2,256]{2,1,0:T(2,128)S(1)} collective-permute-done((f32[12,2,256]{2,1,0:T(2,128)S(1)}, f32[12,2,256]{2,1,0:T(2,128)S(1)}, u32[]{:S(2)}, u32[]{:S(2)}) %collective-permute-start.3) | collective-permute-done | bytes 24608 | tf_op jit(solution)/shard_map/ppermute | solution.py:21
  282.4 16.6 %fusion.62 = f32[8,16,256]{2,1,0:T(8,128)} fusion(f32[8,16,256]{2,1,0:T(8,128)S(1)} %bitcast.106, f32[2,16,256]{2,1,0:T(8,128)S(1)} %collective-permute-done.1, f32[2,16,256]{2,1,0:T(8,128)S(1)} %collective-permute-done, f32[12,18,256]{2,1,0:T(8,128)S(1)} %get-tuple-element.117, f32[12,18,256]{2,1,0:T(8,128)S(1)} %get-tuple-element.116, f32[]{:T(128)} %bitcast.38, ...), kind=kLoop, calls=%fused_computation.80 | loop fusion | flops 1736704 | bytes 2949220 | tf_op jit(solution)/shard_map/add | solution.py:131
  (315 shorter events, 102.7 us)
Async XLA Ops:
  6.5 5.0 %copy-start.1 = (s32[1,1,64]{2,1,0:T(1,128)S(1)}, s32[1,1,64]{2,1,0:T(1,128)}, u32[]{:S(2)}) copy-start(s32[1,1,64]{2,1,0:T(1,128)} %param.12) | copy-start | bytes 772
  6.5 5.1 %copy-start = (s32[1,1,64]{2,1,0:T(1,128)S(1)}, s32[1,1,64]{2,1,0:T(1,128)}, u32[]{:S(2)}) copy-start(s32[1,1,64]{2,1,0:T(1,128)} %param.11) | copy-start | bytes 772
  6.5 145.1 %reduce-scatter.2.cloned.1.call-start = ((), (), s32[]{:S(2)}) async-start(), calls=%async_computation.1 | async-start | bytes 786432 | tf_op jit(solution)/shard_map/reduce_scatter | solution.py:84
  135.1 100.1 %all-reduce.4.cloned.1.call-start = ((), (), s32[]{:S(2)}) async-start(), calls=%async_computation.4 | async-start | bytes 2097152 | tf_op jit(solution)/shard_map/psum | solution.py:104
  156.7 89.3 %all-gather.3.cloned.1.call-start = ((), (), s32[]{:S(2)}) async-start(), calls=%async_computation.2 | async-start | bytes 1572864 | tf_op jit(solution)/shard_map/all_gather | solution.py:109
  237.1 20.5 %all-gather.5.cloned.1.call-start = ((), (), s32[]{:S(2)}) async-start(), calls=%async_computation.3 | async-start | bytes 1572864 | tf_op jit(solution)/shard_map/all_gather | solution.py:110
  246.0 11.6 %copy-start.2 = (f32[512,512]{1,0:T(8,128)S(1)}, f32[512,512]{1,0:T(8,128)}, u32[]{:S(2)}) copy-start(f32[512,512]{1,0:T(8,128)} %all-gather.3.cloned.1.call-done) | copy-start | bytes 3145732
  257.6 2.3 copy-start.3
  264.7 6.7 %copy-start.4 = (f32[5,5]{1,0:T(8,128)S(1)}, f32[5,5]{1,0:T(8,128)}, u32[]{:S(2)}) copy-start(f32[5,5]{1,0:T(8,128)} %param.15) | copy-start | bytes 304
  265.5 6.6 %collective-permute-start.1 = (f32[2,16,256]{2,1,0:T(8,128)S(1)}, f32[2,16,256]{2,1,0:T(8,128)S(1)}, u32[]{:S(2)}, u32[]{:S(2)}) collective-permute-start(f32[2,16,256]{2,1,0:T(8,128)S(1)} %bitcast.115), channel_id=1, source_target_pairs={{4,0},{8,4},{12,8},{5,1},{9,5},{13,9},{6,2},{10,6},{14,10},{7,3},{... | collective-permute-start | bytes 98312 | tf_op jit(solution)/shard_map/ppermute | solution.py:21
  266.8 6.1 %collective-permute-start = (f32[2,16,256]{2,1,0:T(8,128)S(1)}, f32[2,16,256]{2,1,0:T(8,128)S(1)}, u32[]{:S(2)}, u32[]{:S(2)}) collective-permute-start(f32[2,16,256]{2,1,0:T(8,128)S(1)} %bitcast.114), channel_id=1, source_target_pairs={{0,4},{4,8},{8,12},{1,5},{5,9},{9,13},{2,6},{6,10},{10,14},{3,7},{... | collective-permute-start | bytes 98312 | tf_op jit(solution)/shard_map/ppermute | solution.py:20
  272.9 5.6 %collective-permute-start.2 = (f32[12,2,256]{2,1,0:T(2,128)S(1)}, f32[12,2,256]{2,1,0:T(2,128)S(1)}, u32[]{:S(2)}, u32[]{:S(2)}) collective-permute-start(f32[12,2,256]{2,1,0:T(2,128)S(1)} %get-tuple-element.118), channel_id=1, source_target_pairs={{0,2},{1,3},{4,6},{5,7},{8,10},{9,11},{12,14},{13,15},{16,18},{17,... | collective-permute-start | bytes 73736 | tf_op jit(solution)/shard_map/ppermute | solution.py:20
  276.6 5.7 %collective-permute-start.3 = (f32[12,2,256]{2,1,0:T(2,128)S(1)}, f32[12,2,256]{2,1,0:T(2,128)S(1)}, u32[]{:S(2)}, u32[]{:S(2)}) collective-permute-start(f32[12,2,256]{2,1,0:T(2,128)S(1)} %get-tuple-element.119), channel_id=1, source_target_pairs={{2,0},{3,1},{6,4},{7,5},{10,8},{11,9},{14,12},{15,13},{18,16},{19,... | collective-permute-start | bytes 73736 | tf_op jit(solution)/shard_map/ppermute | solution.py:21
Sparse Core Ops, SparseCore 0:
  135.2 16.4 reduce-scatter.1
  156.8 78.3 all-reduce.3
  237.3 8.6 all-gather.2
  247.4 10.1 all-gather.4
where the time goes:
time: 307 us; the launch traced here: 305 us
  local copies, waits for them, and re-layouts  107 us (35%)
  waiting for transfers between devices  92.5 us (30%)
  other arithmetic  31.9 us (10%)
  blocking collectives  23.4 us (8%)
  matrix products  23.2 us (8%)
  between operations  14.8 us (5%)
  starting transfers between devices  11.1 us (4%)
    gather x192, local copies, waits for them, and re-layouts  73 us
    psum x1, waiting for transfers between devices, shards(): lax.psum((gram_real, gram_imag, energy), ('vox', 'chan'))  55.8 us
    psum x1, blocking collectives, shards(): lax.psum((gram_real, gram_imag, energy), ('vox', 'chan'))  21.4 us
    gather x8, local copies, waits for them, and re-layouts, one_turn(): picked = weights[chosen]  17.5 us
    add x1, other arithmetic, shards(): psf_image + psf_kernel[shift_a, shift_b] * padded[shift_a:shift_a + lat_c...  16.6 us
    reduce_scatter x1, waiting for transfers between devices, shards(): lax.psum_scatter(arranged, 'chan', scatter_dimension=1, tiled=True)  16.5 us
    all_gather x1, waiting for transfers between devices, shards(): lax.all_gather(norm_imag, 'frm', axis=0, tiled=True)  8.93 us
    dot_general x8, matrix products, one_turn(): return totals + jnp.einsum('kt,krc->trc', placing, product)  8.92 us
  transfers between devices with their start and end apart: 8, of which 6 were waited for; matrix products, arithmetic and copies ran while one was open for 2% of the time, Pallas kernels for 0%

commit v1 on v0

--- a/solution.py
+++ b/solution.py
@@ -1,7 +1,13 @@
+import functools
+
 import jax
 import jax.numpy as jnp
 from jax import lax
+from jax.experimental import pallas as pl
+from jax.experimental.pallas import tpu as pltpu
 from jax.sharding import PartitionSpec as P
+
+MESH = pl.DeviceIdType.MESH
 
 TBATCH = 8
 LAT_DEV = 8
@@ -55,7 +61,9 @@
         placing = ((tile_goal[chosen][:, None] == target_ids[None, :]) & live_lane[:, None]).astype(
             jnp.float32
         )
-        return totals + jnp.einsum("kt,krc->trc", placing, product)
+        return totals + jnp.einsum(
+            "kt,krc->trc", placing, product, precision=lax.Precision.HIGHEST
+        )
 
     start_totals = jnp.zeros((tiles_out, tile_size, col_count), jnp.float32)
     turn_count = (live_total + TBATCH - 1) // TBATCH
@@ -135,6 +143,276 @@
     return psf_image
 
 
+def split(value):
+    high = value.astype(jnp.bfloat16)
+    return high, (value - high.astype(jnp.float32)).astype(jnp.bfloat16)
+
+
+def beam_kernel(goal_ref, start_ref, live_ref, weights_ref, echo_ref, map_ref, out_ref, operator, high_ref, low_ref):
+    blocks, voxels, tile = operator.shape
+    operator[...] = jnp.zeros_like(operator)
+    lane = lax.broadcasted_iota(jnp.int32, (tile, tile), 1)
+
+    def place(slot, carry):
+        first = start_ref[slot]
+        block = first // tile
+        shift = first - block * tile
+        rows = pl.ds(pl.multiple_of(goal_ref[slot] * tile, tile), tile)
+        turned = pltpu.roll(weights_ref[slot].astype(jnp.float32), shift, 1)
+        operator[block, rows, :] += jnp.where(lane >= shift, turned, 0.0)
+        operator[block + 1, rows, :] += jnp.where(lane < shift, turned, 0.0)
+        return carry
+
+    lax.fori_loop(0, live_ref[0], place, 0)
+    picks = lax.broadcasted_iota(jnp.int32, (voxels, voxels), 0) == map_ref[...]
+    picks = picks.astype(jnp.float32).T.astype(jnp.bfloat16)
+    for block in range(blocks - 1):
+        high, low = split(operator[block])
+        columns = slice(block * tile, (block + 1) * tile)
+        for part, target in ((high, high_ref), (low, low_ref)):
+            moved = jnp.dot(picks, part, preferred_element_type=jnp.float32)
+            target[:, columns] = moved.astype(jnp.bfloat16)
+    sums = jnp.dot(high_ref[...], echo_ref[...], preferred_element_type=jnp.float32)
+    sums += jnp.dot(low_ref[...], echo_ref[...], preferred_element_type=jnp.float32)
+    halves, cells, _ = out_ref.shape
+    width = cells // LAT_DEV
+    for lat in range(LAT_DEV):
+        for half in range(halves):
+            source = (lat * halves + half) * width
+            out_ref[half, lat * width : (lat + 1) * width, :] = sums[source : source + width]
+
+
+def gather_kernel(
+    count, part_ref, out_ref, arrived, once_send, once_recv, own_recv, mate_recv, up_send, down_send, mate_send
+):
+    vox, chan, frm = lax.axis_index("vox"), lax.axis_index("chan"), lax.axis_index("frm")
+    beside, mate = {"chan": 1 - chan}, {"frm": 1 - frm}
+    above, below = {"vox": vox + 1}, {"vox": vox - 1}
+    can_up, can_down = vox + 1 < count, vox > 0
+    barrier = pltpu.get_barrier_semaphore()
+
+    def greet(target):
+        pl.semaphore_signal(barrier, inc=1, device_id=target, device_id_type=MESH)
+
+    greet(beside)
+    greet(mate)
+    pl.when(can_up)(lambda: greet(above))
+    pl.when(can_down)(lambda: greet(below))
+    pl.semaphore_wait(barrier, 4 - jnp.where(can_up, 0, 1) - jnp.where(can_down, 0, 1))
+
+    def remote(source, target, sent, received, device):
+        return pltpu.make_async_remote_copy(
+            src_ref=source, dst_ref=target, send_sem=sent, recv_sem=received, device_id=device, device_id_type=MESH
+        )
+
+    def item(block, side, sent, device):
+        place = out_ref.at[block, side, frm]
+        return remote(place, place, sent, own_recv.at[block, side], device)
+
+    def to_mate(block, side):
+        place = out_ref.at[block, side, frm]
+        return remote(place, place, mate_send.at[block, side], mate_recv.at[block, side], mate)
+
+    def go_up(block, side):
+        return item(block, side, up_send.at[block, side], above)
+
+    def go_down(block, side):
+        return item(block, side, down_send.at[block, side], below)
+
+    def landed(block, side):
+        item(block, side, once_send.at[1], beside).wait_recv()
+
+    swap = remote(part_ref.at[1 - chan], arrived, once_send.at[0], once_recv.at[0], beside)
+    swap.start()
+    swap.wait()
+    out_ref[vox, chan, frm] = (part_ref[chan] + arrived[...]).astype(out_ref.dtype)
+    across = item(vox, chan, once_send.at[1], beside)
+    across.start()
+
+    def spread(side):
+        pl.when(can_up)(lambda: go_up(vox, side).start())
+        pl.when(can_down)(lambda: go_down(vox, side).start())
+        to_mate(vox, side).start()
+
+    spread(chan)
+    landed(vox, 1 - chan)
+    spread(1 - chan)
+    for step in range(1, count):
+        for turn in range(2):
+            side = chan if turn == 0 else 1 - chan
+
+            @pl.when(vox >= step)
+            def _():
+                landed(vox - step, side)
+                pl.when(can_up)(lambda: go_up(vox - step, side).start())
+                to_mate(vox - step, side).start()
+
+            @pl.when(vox + step < count)
+            def _():
+                landed(vox + step, side)
+                pl.when(can_down)(lambda: go_down(vox + step, side).start())
+                to_mate(vox + step, side).start()
+
+    across.wait_send()
+    for block in range(count):
+        for side in range(2):
+            copy = to_mate(block, side)
+            copy.wait_send()
+            place = out_ref.at[block, side, 1 - frm]
+            remote(place, place, mate_send.at[block, side], mate_recv.at[block, side], mate).wait_recv()
+            pl.when(can_up & (vox >= block))(lambda: go_up(block, side).wait_send())
+            pl.when(can_down & (vox <= block))(lambda: go_down(block, side).wait_send())
+
+
+def filter_kernel(count, beams_ref, psf_ref, out_ref, high_ref, low_ref, padded):
+    vox, chan, frm = lax.axis_index("vox"), lax.axis_index("chan"), lax.axis_index("frm")
+    lat, depth, half = out_ref.shape
+    cells = lat * depth
+    pair = 2 * half
+    total = count * 2 * cells
+    left = beams_ref[:, :, 0].reshape(total, pair)
+    right = beams_ref[:, :, 1].reshape(total, pair)
+
+    def gram(first, second):
+        block = lax.dot_general(first, second, (((0,), (0,)), ((), ())), preferred_element_type=jnp.float32)
+        real = block[:half, :half] + block[half:, half:]
+        imag = block[:half, half:] - block[half:, :half]
+        return real, imag
+
+    grams = {(0, 0): gram(left, left), (0, 1): gram(left, right), (1, 1): gram(right, right)}
+    grams[1, 0] = (grams[0, 1][0].T, -grams[0, 1][1].T)
+    eye = lax.broadcasted_iota(jnp.int32, (half, half), 0) == lax.broadcasted_iota(jnp.int32, (half, half), 1)
+    diagonal = jnp.where(eye, grams[0, 0][0] + grams[1, 1][0], 0.0)
+    trace = jnp.sum(jnp.sum(diagonal, axis=0, keepdims=True), axis=1, keepdims=True)
+    factor = (2 * half) / trace
+    for (row, column), (real, imag) in grams.items():
+        real_parts, imag_parts = split(factor * real), split(factor * imag)
+        for target, real_part, imag_part in zip((high_ref, low_ref), real_parts, imag_parts):
+            top, side = row * pair, column * pair
+            target[top : top + half, side : side + half] = real_part
+            target[top : top + half, side + half : side + pair] = imag_part
+            target[top + half : top + pair, side : side + half] = -imag_part
+            target[top + half : top + pair, side + half : side + pair] = real_part
+
+    before, after = jnp.maximum(vox - 1, 0), jnp.minimum(vox + 1, count - 1)
+    edge = 2 * depth
+
+    def both(block, side, rows):
+        return jnp.concatenate([beams_ref[block, side, 0, rows], beams_ref[block, side, 1, rows]], axis=1)
+
+    other = 1 - chan
+    near = jnp.concatenate(
+        [
+            both(before, other, slice(cells - edge, cells)),
+            both(vox, other, slice(0, cells)),
+            both(after, other, slice(0, edge)),
+        ],
+        axis=0,
+    )
+    tall = lat + 4
+    slots = -(-2 * tall // 16) * 16
+    picked = lax.broadcasted_iota(jnp.int32, (slots, tall * depth), 0)
+    source = lax.broadcasted_iota(jnp.int32, (slots, tall * depth), 1)
+    wanted = (picked // 2) * depth + picked % 2 + jnp.where(chan == 0, 0, depth - 2)
+    picks = ((source == wanted) & (picked < 2 * tall)).astype(jnp.float32).astype(jnp.bfloat16)
+    near = jnp.dot(picks, near, preferred_element_type=jnp.float32).astype(jnp.bfloat16)
+    beams = jnp.concatenate(
+        [
+            both(before, chan, slice(cells - edge, cells)),
+            both(vox, chan, slice(0, cells)),
+            both(after, chan, slice(0, edge)),
+            near,
+        ],
+        axis=0,
+    )
+
+    def times(high, low, columns):
+        result = jnp.dot(high, high_ref[:, columns], preferred_element_type=jnp.float32)
+        result += jnp.dot(high, low_ref[:, columns], preferred_element_type=jnp.float32)
+        if low is not None:
+            result += jnp.dot(low, high_ref[:, columns], preferred_element_type=jnp.float32)
+        return result
+
+    echo = beams.astype(jnp.float32)
+    whole = slice(0, 2 * pair)
+    term = POLY_COEFFS[3] * times(beams, None, whole) + POLY_COEFFS[2] * echo
+    term = times(*split(term), whole) + POLY_COEFFS[1] * echo
+    own = pl.ds(pl.multiple_of(frm * pair, pair), pair)
+    echo = jnp.where(frm == 0, echo[:, :pair], echo[:, pair:])
+    term = times(*split(term), own) + POLY_COEFFS[0] * echo
+    envelope = jnp.sqrt(term[:, :half] * term[:, :half] + term[:, half:] * term[:, half:] + 1e-06)
+
+    padded[...] = jnp.zeros_like(padded)
+    has_before, has_after = jnp.where(vox > 0, 1.0, 0.0), jnp.where(vox + 1 < count, 1.0, 0.0)
+    right_side, left_side = jnp.where(chan == 0, 1.0, 0.0), jnp.where(chan == 0, 0.0, 1.0)
+    for line in range(tall):
+        scale = has_before if line < 2 else has_after if line >= lat + 2 else None
+        middle = envelope[line * depth : (line + 1) * depth]
+        start = tall * depth + 2 * line
+        rim = envelope[start : start + 2]
+        if scale is not None:
+            middle, rim = middle * scale, rim * scale
+        padded[line, 8 : 8 + depth, :] = middle
+        padded[line, 6:8, :] = rim * left_side
+        padded[line, 8 + depth : 10 + depth, :] = rim * right_side
+    result = jnp.zeros((lat, depth, half), jnp.float32)
+    for shift_b in range(5):
+        for shift_a in range(5):
+            result += psf_ref[shift_a, shift_b] * padded[shift_a : shift_a + lat, 6 + shift_b : 6 + shift_b + depth]
+    out_ref[...] = result
+
+
+def kernel_shards(count, echo_data, tile_weights, tile_target, tile_offset, tile_count, grid_map, psf_kernel):
+    rows, half = echo_data.shape[2], echo_data.shape[4]
+    slots, tile = tile_weights.shape[2], tile_weights.shape[4]
+    voxels = grid_map.shape[1]
+    cells, pair = voxels // 2, 2 * half
+    depth = cells // LAT_DEV
+    vmem, smem = pl.BlockSpec(memory_space=pltpu.VMEM), pl.BlockSpec(memory_space=pltpu.SMEM)
+    parts = pl.pallas_call(
+        beam_kernel,
+        name="beam",
+        out_shape=jax.ShapeDtypeStruct((2, cells, pair), jnp.float32),
+        in_specs=[smem, smem, smem, vmem, vmem, vmem],
+        out_specs=vmem,
+        scratch_shapes=[
+            pltpu.VMEM((rows // tile + 1, voxels, tile), jnp.float32),
+            pltpu.VMEM((voxels, rows), jnp.bfloat16),
+            pltpu.VMEM((voxels, rows), jnp.bfloat16),
+        ],
+    )(
+        tile_target.reshape(-1),
+        tile_offset.reshape(-1),
+        tile_count.reshape(-1),
+        tile_weights.reshape(slots, tile, tile),
+        echo_data.reshape(rows, pair),
+        grid_map,
+    )
+    pairs = (count, 2)
+    dma = pltpu.SemaphoreType.DMA
+    beams = pl.pallas_call(
+        functools.partial(gather_kernel, count),
+        name="gather",
+        out_shape=jax.ShapeDtypeStruct((count, 2, 2, cells, pair), jnp.bfloat16),
+        in_specs=[vmem],
+        out_specs=vmem,
+        scratch_shapes=[pltpu.VMEM((cells, pair), jnp.float32), dma((2,)), dma((1,))] + [dma(pairs)] * 5,
+        compiler_params=pltpu.CompilerParams(collective_id=0, has_side_effects=True),
+    )(parts)
+    return pl.pallas_call(
+        functools.partial(filter_kernel, count),
+        name="filter",
+        out_shape=jax.ShapeDtypeStruct((LAT_DEV, depth, half), jnp.float32),
+        in_specs=[vmem, smem],
+        out_specs=vmem,
+        scratch_shapes=[
+            pltpu.VMEM((2 * pair, 2 * pair), jnp.bfloat16),
+            pltpu.VMEM((2 * pair, 2 * pair), jnp.bfloat16),
+            pltpu.VMEM((LAT_DEV + 4, depth + 16, half), jnp.float32),
+        ],
+    )(beams, psf_kernel)
+
+
 def solution(mesh):
     in_specs = (
         P(("groups", "vox"), "chan", None, None, "frm"),
@@ -146,4 +424,7 @@
         P(),
     )
     out_specs = P(("groups", "vox"), "chan", "frm")
-    return jax.shard_map(shards, mesh=mesh, in_specs=in_specs, out_specs=out_specs, check_vma=False)
+    body = shards
+    if mesh.shape["chan"] == 2 and mesh.shape["frm"] == 2:
+        body = functools.partial(kernel_shards, mesh.shape["vox"])
+    return jax.shard_map(body, mesh=mesh, in_specs=in_specs, out_specs=out_specs, check_vma=False)

time: 307 us -> 57.9 us (0.19)
  local copies, waits for them, and re-layouts: 107 us -> 2.44 us
  waiting for transfers between devices: 92.5 us -> 0 us
  Pallas kernels: 0 us -> 54.5 us
  other arithmetic: 31.9 us -> 0 us
  blocking collectives: 23.4 us -> 0 us
  matrix products: 23.2 us -> 0 us
  between operations: 14.8 us -> 0.66 us
  starting transfers between devices: 11.1 us -> 0 us
    gather x217 -> x0, local copies, waits for them, and re-layouts: 102 us -> none
    psum x1 -> x0, waiting for transfers between devices: 55.8 us -> none  [shards(): lax.psum((gram_real, gram_imag, energy), ('vox', 'chan'))]
    pallas_call x0 -> x3, Pallas kernels: none -> 54.5 us  [the longest x1 32.9 us: kernel_shards(): pl.pallas_call(functools.partial(gather_kernel, count), name='gather', ou...]
    dot_general x29 -> x0, matrix products: 23.2 us -> none  [the longest x8 8.92 us: one_turn(): return totals + jnp.einsum('kt,krc->trc', placing, product)]
    psum x1 -> x0, blocking collectives: 21.4 us -> none  [shards(): lax.psum((gram_real, gram_imag, energy), ('vox', 'chan'))]
    add x1 -> x0, other arithmetic: 16.6 us -> none  [shards(): psf_image + psf_kernel[shift_a, shift_b] * padded[shift_a:shift_a + lat_c...]
    reduce_scatter x1 -> x0, waiting for transfers between devices: 16.5 us -> none  [shards(): lax.psum_scatter(arranged, 'chan', scatter_dimension=1, tiled=True)]
    all_gather x2 -> x0, waiting for transfers between devices: 15.5 us -> none  [the longest x1 8.93 us: shards(): lax.all_gather(norm_imag, 'frm', axis=0, tiled=True)]
  transfers between devices with their start and end apart: 8 -> 0, of which waited for: 6 -> 0; matrix products, arithmetic and copies ran while one was open for 2% -> 0% of each run, Pallas kernels for 0% -> 0%
where the time goes in v1:
time: 57.9 us; the launch traced here: 57.6 us
  Pallas kernels  54.5 us (94%)
  local copies, waits for them, and re-layouts  2.44 us (4%)
  between operations  0.66 us (1%)
    pallas_call x1, Pallas kernels, kernel_shards(): pl.pallas_call(functools.partial(gather_kernel, count), name='gather', ou...  32.9 us
    pallas_call x1, Pallas kernels, kernel_shards(): pl.pallas_call(functools.partial(filter_kernel, count), name='filter', ou...  11.9 us
    pallas_call x1, Pallas kernels, kernel_shards(): pl.pallas_call(beam_kernel, name='beam', out_shape=jax.ShapeDtypeStruct((...  9.63 us
    unnamed x1, local copies, waits for them, and re-layouts  2.44 us

profile of v1, /device:TPU:0, one launch (start us, length us, event | category | flops | bytes accessed | tf_op | source)
XLA Modules:
  0.0 57.6 jit_solution(15223192315137094016)
XLA Ops:
  0.7 2.4 %copy.8 = bf16[128,8,2,256]{3,1,2,0:T(8,128)(2,1)} copy(bf16[128,8,2,256]{3,2,1,0:T(2,128)(2,1)} %bitcast.10) | data formatting | bytes 2097152
  3.1 9.6 %beam.1.part_ref = f32[2,128,512]{2,1,0:T(8,128)} custom-call(s32[64]{0:T(128)} %bitcast.11, s32[64]{0:T(128)} %bitcast.12, s32[1]{0:T(128)} %bitcast.7.live_ref, bf16[64,128,128]{2,1,0:T(8,128)(2,1)} %bitcast.9, bf16[1024,512]{1,0:T(8,128)(2,1)} %bitcast.8, s32[1,256]{1,0:T(1,128)} %map_ref.1), custom_call_target="tpu_custom_call" | custom-call | tf_op jit(solution)/shard_map/beam/pallas_call | solution.py:372
  12.7 32.9 %gather.1.beams_ref = bf16[4,2,2,128,512]{4,3,2,1,0:T(8,128)(2,1)} custom-call(f32[2,128,512]{2,1,0:T(8,128)} %beam.1.part_ref), custom_call_target="tpu_custom_call" | custom-call | tf_op jit(solution)/shard_map/gather/pallas_call | solution.py:393
  45.7 11.9 %filter.1 = f32[8,16,256]{2,1,0:T(8,128)} custom-call(bf16[4,2,2,128,512]{4,3,2,1,0:T(8,128)(2,1)} %gather.1.beams_ref, f32[5,5]{1,0:T(8,128)} %psf_ref.1), custom_call_target="tpu_custom_call" | custom-call | tf_op jit(solution)/shard_map/filter/pallas_call | solution.py:402

commit v2 on v1

--- a/solution.py
+++ b/solution.py
@@ -8,6 +8,8 @@
 from jax.sharding import PartitionSpec as P
 
 MESH = pl.DeviceIdType.MESH
+PIECES = 4
+GROUP = 8
 
 TBATCH = 8
 LAT_DEV = 8
@@ -148,22 +150,33 @@
     return high, (value - high.astype(jnp.float32)).astype(jnp.bfloat16)
 
 
-def beam_kernel(goal_ref, start_ref, live_ref, weights_ref, echo_ref, map_ref, out_ref, operator, high_ref, low_ref):
+def beam_kernel(goal_ref, start_ref, live_ref, weights_ref, echo_ref, map_ref, out_ref, small_ref, operator, high_ref, low_ref):
     blocks, voxels, tile = operator.shape
     operator[...] = jnp.zeros_like(operator)
     lane = lax.broadcasted_iota(jnp.int32, (tile, tile), 1)
 
-    def place(slot, carry):
-        first = start_ref[slot]
-        block = first // tile
-        shift = first - block * tile
-        rows = pl.ds(pl.multiple_of(goal_ref[slot] * tile, tile), tile)
-        turned = pltpu.roll(weights_ref[slot].astype(jnp.float32), shift, 1)
-        operator[block, rows, :] += jnp.where(lane >= shift, turned, 0.0)
-        operator[block + 1, rows, :] += jnp.where(lane < shift, turned, 0.0)
+    slots = weights_ref.shape[0]
+    live = live_ref[0]
+
+    def place(turn, carry):
+        ready = []
+        for index in range(GROUP):
+            slot = turn * GROUP + index
+            kept = jnp.minimum(slot, slots - 1)
+            first = start_ref[kept]
+            block = first // tile
+            shift = first - block * tile
+            rows = pl.ds(pl.multiple_of(goal_ref[kept] * tile, tile), tile)
+            turned = pltpu.roll(weights_ref[kept].astype(jnp.float32), shift, 1)
+            limit = jnp.where(slot < live, shift, tile)
+            least = jnp.where(slot < live, 0, tile)
+            ready.append((block, rows, jnp.where(lane >= limit, turned, 0.0), turned, shift, least))
+        for block, rows, high, turned, shift, least in ready:
+            operator[block, rows, :] += high
+            operator[block + 1, rows, :] += jnp.where((lane < shift) & (lane >= least), turned, 0.0)
         return carry
 
-    lax.fori_loop(0, live_ref[0], place, 0)
+    lax.fori_loop(0, (live + GROUP - 1) // GROUP, place, 0)
     picks = lax.broadcasted_iota(jnp.int32, (voxels, voxels), 0) == map_ref[...]
     picks = picks.astype(jnp.float32).T.astype(jnp.bfloat16)
     for block in range(blocks - 1):
@@ -179,16 +192,20 @@
     for lat in range(LAT_DEV):
         for half in range(halves):
             source = (lat * halves + half) * width
-            out_ref[half, lat * width : (lat + 1) * width, :] = sums[source : source + width]
+            chosen = sums[source : source + width]
+            out_ref[half, lat * width : (lat + 1) * width, :] = chosen
+            small_ref[half, lat * width : (lat + 1) * width, :] = chosen.astype(small_ref.dtype)
 
 
 def gather_kernel(
-    count, part_ref, out_ref, arrived, once_send, once_recv, own_recv, mate_recv, up_send, down_send, mate_send
+    count, part_ref, small_ref, out_ref, arrived, swap_send, swap_recv, own_recv, mate_recv, up_send, down_send, mate_send
 ):
     vox, chan, frm = lax.axis_index("vox"), lax.axis_index("chan"), lax.axis_index("frm")
     beside, mate = {"chan": 1 - chan}, {"frm": 1 - frm}
     above, below = {"vox": vox + 1}, {"vox": vox - 1}
     can_up, can_down = vox + 1 < count, vox > 0
+    pieces = swap_send.shape[0]
+    height = part_ref.shape[1] // pieces
     barrier = pltpu.get_barrier_semaphore()
 
     def greet(target):
@@ -205,63 +222,63 @@
             src_ref=source, dst_ref=target, send_sem=sent, recv_sem=received, device_id=device, device_id_type=MESH
         )
 
-    def item(block, side, sent, device):
-        place = out_ref.at[block, side, frm]
-        return remote(place, place, sent, own_recv.at[block, side], device)
-
-    def to_mate(block, side):
-        place = out_ref.at[block, side, frm]
-        return remote(place, place, mate_send.at[block, side], mate_recv.at[block, side], mate)
-
-    def go_up(block, side):
-        return item(block, side, up_send.at[block, side], above)
-
-    def go_down(block, side):
-        return item(block, side, down_send.at[block, side], below)
-
-    def landed(block, side):
-        item(block, side, once_send.at[1], beside).wait_recv()
-
-    swap = remote(part_ref.at[1 - chan], arrived, once_send.at[0], once_recv.at[0], beside)
-    swap.start()
-    swap.wait()
-    out_ref[vox, chan, frm] = (part_ref[chan] + arrived[...]).astype(out_ref.dtype)
-    across = item(vox, chan, once_send.at[1], beside)
-    across.start()
-
-    def spread(side):
-        pl.when(can_up)(lambda: go_up(vox, side).start())
-        pl.when(can_down)(lambda: go_down(vox, side).start())
-        to_mate(vox, side).start()
-
-    spread(chan)
-    landed(vox, 1 - chan)
-    spread(1 - chan)
-    for step in range(1, count):
-        for turn in range(2):
-            side = chan if turn == 0 else 1 - chan
-
-            @pl.when(vox >= step)
-            def _():
-                landed(vox - step, side)
-                pl.when(can_up)(lambda: go_up(vox - step, side).start())
-                to_mate(vox - step, side).start()
-
-            @pl.when(vox + step < count)
-            def _():
-                landed(vox + step, side)
-                pl.when(can_down)(lambda: go_down(vox + step, side).start())
-                to_mate(vox + step, side).start()
-
-    across.wait_send()
-    for block in range(count):
-        for side in range(2):
-            copy = to_mate(block, side)
-            copy.wait_send()
-            place = out_ref.at[block, side, 1 - frm]
-            remote(place, place, mate_send.at[block, side], mate_recv.at[block, side], mate).wait_recv()
-            pl.when(can_up & (vox >= block))(lambda: go_up(block, side).wait_send())
-            pl.when(can_down & (vox <= block))(lambda: go_down(block, side).wait_send())
+    def rows(piece):
+        return pl.ds(piece * height, height)
+
+    def item(block, piece, sent, device):
+        place = out_ref.at[block, frm, :, rows(piece)]
+        return remote(place, place, sent, own_recv.at[block, piece], device)
+
+    def to_mate(block, piece, owner=None):
+        place = out_ref.at[block, frm if owner is None else owner, :, rows(piece)]
+        return remote(place, place, mate_send.at[block, piece], mate_recv.at[block, piece], mate)
+
+    def go_up(block, piece):
+        return item(block, piece, up_send.at[block, piece], above)
+
+    def go_down(block, piece):
+        return item(block, piece, down_send.at[block, piece], below)
+
+    def swap(piece):
+        return remote(
+            small_ref.at[:, rows(piece)], arrived.at[:, rows(piece)], swap_send.at[piece], swap_recv.at[piece], beside
+        )
+
+    def relay(step, piece):
+        @pl.when(vox >= step)
+        def _():
+            item(vox - step, piece, up_send.at[0, piece], above).wait_recv()
+            pl.when(can_up)(lambda: go_up(vox - step, piece).start())
+            to_mate(vox - step, piece).start()
+
+        @pl.when(vox + step < count)
+        def _():
+            item(vox + step, piece, down_send.at[0, piece], below).wait_recv()
+            pl.when(can_down)(lambda: go_down(vox + step, piece).start())
+            to_mate(vox + step, piece).start()
+
+    for piece in range(pieces):
+        swap(piece).start()
+    for wave in range(pieces + count - 1):
+        if wave < pieces:
+            swap(wave).wait_recv()
+            mine = part_ref[:, rows(wave)] + arrived[:, rows(wave)].astype(jnp.float32)
+            out_ref[vox, frm, :, rows(wave)] = mine.astype(out_ref.dtype)
+            pl.when(can_up)(lambda: go_up(vox, wave).start())
+            pl.when(can_down)(lambda: go_down(vox, wave).start())
+            to_mate(vox, wave).start()
+        for step in range(1, count):
+            piece = wave - step
+            if 0 <= piece < pieces:
+                relay(step, piece)
+
+    for piece in range(pieces):
+        swap(piece).wait_send()
+        for block in range(count):
+            to_mate(block, piece).wait_send()
+            to_mate(block, piece, 1 - frm).wait_recv()
+            pl.when(can_up & (vox >= block))(lambda: go_up(block, piece).wait_send())
+            pl.when(can_down & (vox <= block))(lambda: go_down(block, piece).wait_send())
 
 
 def filter_kernel(count, beams_ref, psf_ref, out_ref, high_ref, low_ref, padded):
@@ -270,8 +287,8 @@
     cells = lat * depth
     pair = 2 * half
     total = count * 2 * cells
-    left = beams_ref[:, :, 0].reshape(total, pair)
-    right = beams_ref[:, :, 1].reshape(total, pair)
+    left = beams_ref[:, 0].reshape(total, pair)
+    right = beams_ref[:, 1].reshape(total, pair)
 
     def gram(first, second):
         block = lax.dot_general(first, second, (((0,), (0,)), ((), ())), preferred_element_type=jnp.float32)
@@ -298,7 +315,7 @@
     edge = 2 * depth
 
     def both(block, side, rows):
-        return jnp.concatenate([beams_ref[block, side, 0, rows], beams_ref[block, side, 1, rows]], axis=1)
+        return jnp.concatenate([beams_ref[block, 0, side, rows], beams_ref[block, 1, side, rows]], axis=1)
 
     other = 1 - chan
     near = jnp.concatenate(
@@ -326,20 +343,17 @@
         axis=0,
     )
 
-    def times(high, low, columns):
-        result = jnp.dot(high, high_ref[:, columns], preferred_element_type=jnp.float32)
-        result += jnp.dot(high, low_ref[:, columns], preferred_element_type=jnp.float32)
-        if low is not None:
-            result += jnp.dot(low, high_ref[:, columns], preferred_element_type=jnp.float32)
-        return result
+    def times(left, right_ref, columns):
+        return jnp.dot(left, right_ref[:, columns], preferred_element_type=jnp.float32)
 
     echo = beams.astype(jnp.float32)
     whole = slice(0, 2 * pair)
-    term = POLY_COEFFS[3] * times(beams, None, whole) + POLY_COEFFS[2] * echo
-    term = times(*split(term), whole) + POLY_COEFFS[1] * echo
+    term = POLY_COEFFS[3] * times(beams, high_ref, whole) + POLY_COEFFS[2] * echo
+    term = times(term.astype(jnp.bfloat16), high_ref, whole) + POLY_COEFFS[1] * echo
     own = pl.ds(pl.multiple_of(frm * pair, pair), pair)
     echo = jnp.where(frm == 0, echo[:, :pair], echo[:, pair:])
-    term = times(*split(term), own) + POLY_COEFFS[0] * echo
+    high, low = split(term)
+    term = times(high, high_ref, own) + times(high, low_ref, own) + times(low, high_ref, own) + POLY_COEFFS[0] * echo
     envelope = jnp.sqrt(term[:, :half] * term[:, :half] + term[:, half:] * term[:, half:] + 1e-06)
 
     padded[...] = jnp.zeros_like(padded)
@@ -369,12 +383,15 @@
     cells, pair = voxels // 2, 2 * half
     depth = cells // LAT_DEV
     vmem, smem = pl.BlockSpec(memory_space=pltpu.VMEM), pl.BlockSpec(memory_space=pltpu.SMEM)
-    parts = pl.pallas_call(
+    parts, small = pl.pallas_call(
         beam_kernel,
         name="beam",
-        out_shape=jax.ShapeDtypeStruct((2, cells, pair), jnp.float32),
+        out_shape=[
+            jax.ShapeDtypeStruct((2, cells, pair), jnp.float32),
+            jax.ShapeDtypeStruct((2, cells, pair), jnp.bfloat16),
+        ],
         in_specs=[smem, smem, smem, vmem, vmem, vmem],
-        out_specs=vmem,
+        out_specs=[vmem, vmem],
         scratch_shapes=[
             pltpu.VMEM((rows // tile + 1, voxels, tile), jnp.float32),
             pltpu.VMEM((voxels, rows), jnp.bfloat16),
@@ -388,17 +405,18 @@
         echo_data.reshape(rows, pair),
         grid_map,
     )
-    pairs = (count, 2)
+    pieces = PIECES
+    each = (count, pieces)
     dma = pltpu.SemaphoreType.DMA
     beams = pl.pallas_call(
         functools.partial(gather_kernel, count),
         name="gather",
         out_shape=jax.ShapeDtypeStruct((count, 2, 2, cells, pair), jnp.bfloat16),
-        in_specs=[vmem],
+        in_specs=[vmem, vmem],
         out_specs=vmem,
-        scratch_shapes=[pltpu.VMEM((cells, pair), jnp.float32), dma((2,)), dma((1,))] + [dma(pairs)] * 5,
+        scratch_shapes=[pltpu.VMEM((2, cells, pair), jnp.bfloat16)] + [dma((pieces,))] * 2 + [dma(each)] * 5,
         compiler_params=pltpu.CompilerParams(collective_id=0, has_side_effects=True),
-    )(parts)
+    )(parts, small)
     return pl.pallas_call(
         functools.partial(filter_kernel, count),
         name="filter",

time: 57.9 us -> 47.4 us (0.82)
  Pallas kernels: 54.5 us -> 44.3 us
    pallas_call x1, Pallas kernels: 9.63 us -> 4.76 us  [kernel_shards(): pl.pallas_call(beam_kernel, name='beam', out_shape=[jax.ShapeDtypeStruct(...]
    pallas_call x1, Pallas kernels: 11.9 us -> 8.5 us  [kernel_shards(): pl.pallas_call(functools.partial(filter_kernel, count), name='filter', ou...]
    pallas_call x1, Pallas kernels: 32.9 us -> 31 us  [kernel_shards(): pl.pallas_call(functools.partial(gather_kernel, count), name='gather', ou...]
where the time goes in v2:
time: 47.4 us
  Pallas kernels  44.3 us (93%)
  local copies, waits for them, and re-layouts  2.44 us (5%)
  between operations  0.66 us (1%)
    pallas_call x1, Pallas kernels, kernel_shards(): pl.pallas_call(functools.partial(gather_kernel, count), name='gather', ou...  31 us
    pallas_call x1, Pallas kernels, kernel_shards(): pl.pallas_call(functools.partial(filter_kernel, count), name='filter', ou...  8.5 us
    pallas_call x1, Pallas kernels, kernel_shards(): pl.pallas_call(beam_kernel, name='beam', out_shape=[jax.ShapeDtypeStruct(...  4.76 us
    unnamed x1, local copies, waits for them, and re-layouts  2.44 us

profile of v2, /device:TPU:0, one launch (start us, length us, event | category | flops | bytes accessed | tf_op | source)
XLA Modules:
  0.0 47.4 jit_solution(3805941769838470739)
XLA Ops:
  0.7 2.4 %copy.8 = bf16[128,8,2,256]{3,1,2,0:T(8,128)(2,1)} copy(bf16[128,8,2,256]{3,2,1,0:T(2,128)(2,1)} %bitcast.10) | data formatting | bytes 2097152
  3.1 4.8 %beam.1 = (f32[2,128,512]{2,1,0:T(8,128)}, bf16[2,128,512]{2,1,0:T(8,128)(2,1)}) custom-call(s32[64]{0:T(128)} %bitcast.11, s32[64]{0:T(128)} %bitcast.12, s32[1]{0:T(128)} %bitcast.7.live_ref, bf16[64,128,128]{2,1,0:T(8,128)(2,1)} %bitcast.9, bf16[1024,512]{1,0:T(8,128)(2,1)} %bitcast.8, s32[1,256]{1,0:T(1,128)} %map_ref.1), custom_call_target="tpu_custom_call" | custom-call | tf_op jit(solution)/shard_map/beam/pallas_call | solution.py:386
  7.9 31.0 %gather.1.beams_ref = bf16[4,2,2,128,512]{4,3,2,1,0:T(8,128)(2,1)} custom-call(f32[2,128,512]{2,1,0:T(8,128)} %get-tuple-element.7.part_ref, bf16[2,128,512]{2,1,0:T(8,128)(2,1)} %get-tuple-element.8.small_ref), custom_call_target="tpu_custom_call" | custom-call | tf_op jit(solution)/shard_map/gather/pallas_call | solution.py:411
  38.9 8.5 %filter.1 = f32[8,16,256]{2,1,0:T(8,128)} custom-call(bf16[4,2,2,128,512]{4,3,2,1,0:T(8,128)(2,1)} %gather.1.beams_ref, f32[5,5]{1,0:T(8,128)} %psf_ref.1), custom_call_target="tpu_custom_call" | custom-call | tf_op jit(solution)/shard_map/filter/pallas_call | solution.py:420

commit v3 on v2

--- a/solution.py
+++ b/solution.py
@@ -150,15 +150,29 @@
     return high, (value - high.astype(jnp.float32)).astype(jnp.bfloat16)
 
 
-def beam_kernel(goal_ref, start_ref, live_ref, weights_ref, echo_ref, map_ref, out_ref, small_ref, operator, high_ref, low_ref):
+def beam_kernel(goal_ref, start_ref, live_ref, weights_hbm, echo_hbm, map_ref, out_ref, small_ref, operator, high_ref, low_ref, weights_ref, echo_ref, weights_sem, echo_sem):
     blocks, voxels, tile = operator.shape
+    slots = weights_ref.shape[0]
+    live = live_ref[0]
+    turns = (live + GROUP - 1) // GROUP
+
+    def fetch(turn):
+        chunk = pl.ds(turn * GROUP, GROUP)
+        return pltpu.make_async_copy(weights_hbm.at[chunk], weights_ref.at[chunk], weights_sem.at[turn])
+
+    def begin(turn, carry):
+        fetch(turn).start()
+        return carry
+
+    lax.fori_loop(0, turns, begin, 0)
+    echo_copy = pltpu.make_async_copy(echo_hbm, echo_ref, echo_sem.at[0])
+    echo_copy.start()
     operator[...] = jnp.zeros_like(operator)
     lane = lax.broadcasted_iota(jnp.int32, (tile, tile), 1)
 
-    slots = weights_ref.shape[0]
-    live = live_ref[0]
 
     def place(turn, carry):
+        fetch(turn).wait()
         ready = []
         for index in range(GROUP):
             slot = turn * GROUP + index
@@ -176,7 +190,7 @@
             operator[block + 1, rows, :] += jnp.where((lane < shift) & (lane >= least), turned, 0.0)
         return carry
 
-    lax.fori_loop(0, (live + GROUP - 1) // GROUP, place, 0)
+    lax.fori_loop(0, turns, place, 0)
     picks = lax.broadcasted_iota(jnp.int32, (voxels, voxels), 0) == map_ref[...]
     picks = picks.astype(jnp.float32).T.astype(jnp.bfloat16)
     for block in range(blocks - 1):
@@ -185,6 +199,7 @@
         for part, target in ((high, high_ref), (low, low_ref)):
             moved = jnp.dot(picks, part, preferred_element_type=jnp.float32)
             target[:, columns] = moved.astype(jnp.bfloat16)
+    echo_copy.wait()
     sums = jnp.dot(high_ref[...], echo_ref[...], preferred_element_type=jnp.float32)
     sums += jnp.dot(low_ref[...], echo_ref[...], preferred_element_type=jnp.float32)
     halves, cells, _ = out_ref.shape
@@ -383,6 +398,7 @@
     cells, pair = voxels // 2, 2 * half
     depth = cells // LAT_DEV
     vmem, smem = pl.BlockSpec(memory_space=pltpu.VMEM), pl.BlockSpec(memory_space=pltpu.SMEM)
+    hbm = pl.BlockSpec(memory_space=pl.ANY)
     parts, small = pl.pallas_call(
         beam_kernel,
         name="beam",
@@ -390,12 +406,16 @@
             jax.ShapeDtypeStruct((2, cells, pair), jnp.float32),
             jax.ShapeDtypeStruct((2, cells, pair), jnp.bfloat16),
         ],
-        in_specs=[smem, smem, smem, vmem, vmem, vmem],
+        in_specs=[smem, smem, smem, hbm, hbm, vmem],
         out_specs=[vmem, vmem],
         scratch_shapes=[
             pltpu.VMEM((rows // tile + 1, voxels, tile), jnp.float32),
             pltpu.VMEM((voxels, rows), jnp.bfloat16),
             pltpu.VMEM((voxels, rows), jnp.bfloat16),
+            pltpu.VMEM((slots, tile, tile), jnp.bfloat16),
+            pltpu.VMEM((rows, pair), jnp.bfloat16),
+            pltpu.SemaphoreType.DMA((slots // GROUP,)),
+            pltpu.SemaphoreType.DMA((1,)),
         ],
     )(
         tile_target.reshape(-1),

time: 47.4 us -> 47.6 us (level)
    pallas_call x1, Pallas kernels: 31 us -> 30.2 us  [kernel_shards(): pl.pallas_call(functools.partial(gather_kernel, count), name='gather', ou...]
    pallas_call x1, Pallas kernels: 4.76 us -> 5.52 us  [kernel_shards(): pl.pallas_call(beam_kernel, name='beam', out_shape=[jax.ShapeDtypeStruct(...]
where the time goes in v3:
time: 47.6 us; the launch traced here: 47.3 us
  Pallas kernels  44.2 us (93%)
  local copies, waits for them, and re-layouts  2.44 us (5%)
  between operations  0.67 us (1%)
    pallas_call x1, Pallas kernels, kernel_shards(): pl.pallas_call(functools.partial(gather_kernel, count), name='gather', ou...  30.2 us
    pallas_call x1, Pallas kernels, kernel_shards(): pl.pallas_call(functools.partial(filter_kernel, count), name='filter', ou...  8.5 us
    pallas_call x1, Pallas kernels, kernel_shards(): pl.pallas_call(beam_kernel, name='beam', out_shape=[jax.ShapeDtypeStruct(...  5.52 us
    unnamed x1, local copies, waits for them, and re-layouts  2.44 us

profile of v3, /device:TPU:0, one launch (start us, length us, event | category | flops | bytes accessed | tf_op | source)
XLA Modules:
  0.0 47.3 jit_solution(14476308983254176921)
XLA Ops:
  0.7 2.4 %copy.8 = bf16[128,8,2,256]{3,1,2,0:T(8,128)(2,1)} copy(bf16[128,8,2,256]{3,2,1,0:T(2,128)(2,1)} %bitcast.10) | data formatting | bytes 2097152
  3.1 5.5 %beam.1 = (f32[2,128,512]{2,1,0:T(8,128)}, bf16[2,128,512]{2,1,0:T(8,128)(2,1)}) custom-call(s32[64]{0:T(128)} %bitcast.11, s32[64]{0:T(128)} %bitcast.12, s32[1]{0:T(128)} %bitcast.7.live_ref, bf16[64,128,128]{2,1,0:T(8,128)(2,1)} %bitcast.9, bf16[1024,512]{1,0:T(8,128)(2,1)} %bitcast.8, s32[1,256]{1,0:T(1,128)} %map_ref.1), custom_call_target="tpu_custom_call" | custom-call | tf_op jit(solution)/shard_map/beam/pallas_call | solution.py:402
  8.6 30.2 %gather.1.beams_ref = bf16[4,2,2,128,512]{4,3,2,1,0:T(8,128)(2,1)} custom-call(f32[2,128,512]{2,1,0:T(8,128)} %get-tuple-element.7.part_ref, bf16[2,128,512]{2,1,0:T(8,128)(2,1)} %get-tuple-element.8.small_ref), custom_call_target="tpu_custom_call" | custom-call | tf_op jit(solution)/shard_map/gather/pallas_call | solution.py:431
  38.8 8.5 %filter.1 = f32[8,16,256]{2,1,0:T(8,128)} custom-call(bf16[4,2,2,128,512]{4,3,2,1,0:T(8,128)(2,1)} %gather.1.beams_ref, f32[5,5]{1,0:T(8,128)} %psf_ref.1), custom_call_target="tpu_custom_call" | custom-call | tf_op jit(solution)/shard_map/filter/pallas_call | solution.py:440
